TPU v7x, 256 devices: a whole 4x4x8 slice. The times are simulated.
256 devices in a mesh: expert: 32 (over z, x), col: 8 (over y, core).
Axes of the slice: x: 4, y: 4, z: 8, core: 2. Of those that a mesh axis runs over, the one named last changes fastest.
Arguments:
- tokens: bfloat16 [4096, 4096], P('expert', 'col'), may hold values from -6 to 6
- routes: int32 [4096, 8], P('expert'), may hold values from 0 to 63, all different within a row; in each aligned block of 128 rows (0 to 127, 128 to 255, ...) at most 24 rows name the same one
- route_weight: float32 [4096, 8], P('expert'), may hold values from 0.02 to 0.25
- language: int32 [4096], P('expert'), may hold values from 0 to 118
- lang_weight: float32 [119], replicated, may hold values from 0.01 to 0.1
- w_gate: bfloat16 [64, 1536, 4096], P('expert', 'col'), may hold values from -0.09375 to 0.09375
- w_up: bfloat16 [64, 1536, 4096], P('expert', 'col'), may hold values from -0.09375 to 0.09375
- w_down: bfloat16 [64, 1536, 4096], P('expert', None, 'col'), may hold values from -0.15625 to 0.15625
Outputs:
- layer_out: bfloat16 [4096, 4096], P('expert', 'col')
- gram: float32 [64, 1536, 1536], P('expert', 'col')
Inputs may be any that keep to these rules, and one draw needn't show every extreme that they name: `routes`: each row names 8 different experts. In each aligned block of 128 rows no expert is named by more than 24 rows, a bound that some block reaches.
All inputs are finite; a program needn't handle non-finite values.
Results may differ from a plain program's by a relative error of at most 0.0063.
Values may be sent and summed in bfloat16 or wider, within the bound.
A program may use at most 128 MiB of HBM per device.

v0:
```python
import jax
import jax.numpy as jnp
from jax import lax
from jax.sharding import PartitionSpec as P


def on_device(tokens, routes, route_weight, language, lang_weight, w_gate, w_up, w_down):
    tok_rows = routes.shape[0]
    top_count = routes.shape[1]
    local_exp = w_gate.shape[0]
    owners = lax.axis_size("expert")
    experts = local_exp * owners
    capacity = tok_rows * top_count * 3 // (2 * experts)
    expert_ids = jnp.arange(experts, dtype=jnp.int32)
    chosen = routes[:, :, None] == expert_ids[None, None, :]
    hits = jnp.any(chosen, axis=1).astype(jnp.int32)
    coefs = jnp.sum(jnp.where(chosen, route_weight[:, :, None], jnp.zeros((), jnp.float32)), axis=1)
    places = jnp.cumsum(hits, axis=0) - hits
    slot_ids = jnp.arange(capacity, dtype=jnp.int32)
    picks = (hits.T[:, None, :] == 1) & (places.T[:, None, :] == slot_ids[None, :, None])
    row_index = jnp.arange(tok_rows, dtype=jnp.int32)
    slot_token = jnp.sum(jnp.where(picks, row_index[None, None, :], 0), axis=2)
    filled = jnp.any(picks, axis=2)
    lang_table = language[:, None] == jnp.arange(lang_weight.shape[0], dtype=jnp.int32)[None, :]
    calib = jnp.sum(
        jnp.where(lang_table, lang_weight[None, :], jnp.zeros((), jnp.float32)), axis=1
    ).astype(jnp.bfloat16)
    slot_cal = jnp.where(filled, calib[slot_token], jnp.zeros((), jnp.bfloat16)).reshape(
        owners, local_exp, capacity
    )
    slot_coef = jnp.where(
        filled, jnp.take_along_axis(coefs.T, slot_token, axis=1), jnp.zeros((), jnp.float32)
    )
    flat_token = slot_token.reshape(-1)
    flat_filled = filled.reshape(-1)
    whole = lax.all_gather(tokens, "col", axis=1, tiled=True)
    rows = jnp.take(whole, flat_token, axis=0)
    rows = jnp.where(flat_filled[:, None], rows, jnp.zeros((), jnp.bfloat16))
    arrived = lax.all_to_all(
        rows.reshape(owners, local_exp, capacity, whole.shape[1]),
        "expert",
        split_axis=0,
        concat_axis=0,
        tiled=True,
    )
    arrived_cal = lax.all_to_all(slot_cal, "expert", split_axis=0, concat_axis=0, tiled=True)
    gate = jnp.einsum("seck,efk->escf", arrived, w_gate, preferred_element_type=jnp.float32)
    upper = jnp.einsum("seck,efk->escf", arrived, w_up, preferred_element_type=jnp.float32)
    hidden = (jax.nn.silu(gate) * upper).astype(jnp.bfloat16)
    cal_rows = jnp.transpose(arrived_cal, (1, 0, 2))
    scaled = (cal_rows[..., None].astype(jnp.float32) * hidden.astype(jnp.float32)).astype(
        jnp.bfloat16
    )
    d_local = w_down.shape[2]
    piece = lax.all_gather(hidden, "col", axis=3, tiled=True)
    block = jnp.einsum("escu,escv->euv", scaled, piece, preferred_element_type=jnp.float32)
    mixed_now = jnp.einsum("escv,evd->escd", piece, w_down, preferred_element_type=jnp.float32)
    expert_out = mixed_now.astype(jnp.bfloat16)
    returned = lax.all_to_all(expert_out, "expert", split_axis=1, concat_axis=0, tiled=True)
    returned = returned.reshape(experts * capacity, d_local).astype(jnp.float32)
    combined = jnp.zeros((tok_rows, d_local), jnp.float32)
    combined = combined.at[flat_token].add(slot_coef.reshape(-1)[:, None] * returned)
    return (combined.astype(jnp.bfloat16), block)


def solution(mesh):
    in_specs = (
        P("expert", "col"),
        P("expert", None),
        P("expert", None),
        P("expert"),
        P(),
        P("expert", "col", None),
        P("expert", "col", None),
        P("expert", None, "col"),
    )
    out_specs = (P("expert", "col"), P("expert", "col", None))
    return jax.shard_map(
        on_device, mesh=mesh, in_specs=in_specs, out_specs=out_specs, check_vma=False
    )
```

profile of v0, /device:TPU:4, one launch (start us, length us, event | category | flops | bytes accessed | tf_op | source)
XLA Modules:
  0.0 570.8 jit_solution(8276990550696766480)
XLA Ops:
  7.2 0.7 all-gather.3.cloned.1.call-update
  8.0 0.9 fusion.18
  8.8 0.1 copy.38
  9.0 0.1 copy.39
  9.1 0.2 reduce_window_sum.11
  9.3 1.2 select_reduce_fusion
  10.5 0.1 reshape.116
  10.6 1.2 fusion.17
  11.9 26.8 %all-gather.3.cloned.1.call-done = bf16[128,4096]{1,0:T(8,128)(2,1)} async-done(((bf16[128,512]{1,0:T(8,128)(2,1)}), bf16[128,4096]{1,0:T(8,128)(2,1)}) %all-gather.3.cloned.1.call-update) | async-done | bytes 1048592 | tf_op jit(solution)/shard_map/all_gather | solution.py:36
  38.8 23.4 %gather_fusion = bf16[1536,4096]{1,0:T(8,128)(2,1)} fusion(bf16[128,4096]{1,0:T(8,128)(2,1)} %all-gather.3.cloned.1.call-done, s32[2048]{0:T(1024)S(1)} %pad_clamp_fusion.1), kind=kCustom, calls=%fused_computation | custom fusion | bytes 25171968 | tf_op jit(solution)/shard_map/jit(_take)/gather | solution.py:37
  62.2 6.7 %select_select_fusion = bf16[32,2,24,4096]{3,2,1,0:T(8,128)(2,1)S(1)} fusion(bf16[32,2,24,4096]{3,2,1,0:T(8,128)(2,1)} %bitcast.49, pred[32,2,24]{2,1,0:T(4,128)(4,1)S(1)} %compare_and_fusion, pred[32,2,24]{2,1,0:T(4,128)(4,1)S(1)} %broadcast_in_dim.95), kind=kLoop, calls=%fused_computation.4 | loop fusion | flops 12582912 | bytes 25168896 | tf_op jit(solution)/shard_map/jit(_where)/select_n | solution.py:38
  68.9 285.7 %all_to_all.19 = bf16[32,2,24,4096]{3,2,1,0:T(8,128)(2,1)} all-to-all(bf16[32,2,24,4096]{3,2,1,0:T(8,128)(2,1)S(1)} %select_select_fusion), channel_id=1, replica_groups=mesh['expert'=32,'col'=8] {'expert'}, dimensions={0} | all-to-all | bytes 25165824 | tf_op jit(solution)/shard_map/all_to_all | solution.py:39
  354.6 10.1 %fusion.2 = f32[2,32,24,192]{3,2,1,0:T(8,128)} fusion(bf16[32,2,24,4096]{3,2,1,0:T(8,128)(2,1)} %all_to_all.19, bf16[2,192,4096]{2,1,0:T(8,128)(2,1)} %param.13), kind=kOutput, calls=%fused_computation.7 | convolution fusion | flops 2415919104 | bytes 16908288 | tf_op jit(solution)/shard_map/seck,efk->escf/dot_general | solution.py:47
  364.7 10.5 %multiply_convert_fusion.1 = bf16[2,32,24,192]{3,2,1,0:T(8,128)(2,1)} fusion(f32[2,32,24,192]{3,2,1,0:T(8,128)} %fusion.2, bf16[2,192,4096]{2,1,0:T(8,128)(2,1)} %param.14, bf16[32,2,24,4096]{3,2,1,0:T(8,128)(2,1)} %all_to_all.19), kind=kOutput, calls=%fused_computation.18 | convolution fusion | flops 2417688576 | bytes 17498112 | tf_op jit(solution)/shard_map/seck,efk->escf/dot_general | solution.py:48
  375.1 3.7 copy.44
  379.0 0.1 select_reduce_fusion.2
  379.1 9.0 %gather_fusion.1 = bf16[1536]{0:T(1024)(128)(2,1)S(1)} fusion(bf16[128]{0:T(256)(128)(2,1)S(1)} %select_reduce_fusion.2, s32[2048]{0:T(1024)S(1)} %pad_clamp_fusion), kind=kCustom, calls=%fused_computation.1 | custom fusion | bytes 12288 | tf_op jit(solution)/shard_map/gather | solution.py:28
  388.2 0.6 broadcast_select_fusion
  388.8 5.5 all-to-all-start.2
  394.4 76.2 %all-gather.5.cloned.1.call-done = bf16[2,32,24,1536]{1,2,0,3:T(8,128)(2,1)} async-done(((bf16[2,32,24,192]{1,2,0,3:T(8,128)(2,1)}), bf16[2,32,24,1536]{1,2,0,3:T(8,128)(2,1)}) %all-gather.5.cloned.1.call-update) | async-done | bytes 4718608 | tf_op jit(solution)/shard_map/all_gather | solution.py:55
  470.6 22.1 %copy.45 = bf16[2,32,24,1536]{3,2,1,0:T(8,128)(2,1)} copy(bf16[2,32,24,1536]{1,2,0,3:T(8,128)(2,1)} %all-gather.5.cloned.1.call-done) | data formatting | bytes 9437184 | tf_op jit(solution)/shard_map/all_gather | solution.py:55
  492.7 5.0 fusion.8
  497.8 1.3 copy.46
  499.1 10.2 %all-to-all-start.1 = ((bf16[2,32,24,512]{3,2,0,1:T(8,128)(2,1)}), bf16[2,32,24,512]{3,2,0,1:T(8,128)(2,1)}, u32[]{:S(2)}, u32[]{:S(2)}) async-start(bf16[2,32,24,512]{3,2,0,1:T(8,128)(2,1)} %copy.46), calls=%async_computation.1 | async-start | bytes 3145728 | tf_op jit(solution)/shard_map/all_to_all | solution.py:59
  509.3 0.1 reduce_or.22
  509.7 10.7 %gather_fusion.2 = f32[1536]{0:T(1024)S(1)} fusion(f32[64,128]{0,1:T(8,128)S(1)} %bitcast.48, s32[1536]{0:T(1024)S(1)} %reshape.137), kind=kCustom, calls=%fused_computation.2 | custom fusion | bytes 24576 | tf_op jit(solution)/shard_map/jit(take_along_axis)/gather | solution.py:32
  520.5 5.2 convolution_bitcast_fusion
  525.6 23.4 %all-to-all-done.1 = bf16[2,32,24,512]{3,2,0,1:T(8,128)(2,1)} async-done(((bf16[2,32,24,512]{3,2,0,1:T(8,128)(2,1)}), bf16[2,32,24,512]{3,2,0,1:T(8,128)(2,1)}, u32[]{:S(2)}, u32[]{:S(2)}) %all-to-all-start.1) | async-done | bytes 1572896 | tf_op jit(solution)/shard_map/all_to_all | solution.py:59
  549.1 1.8 bitcast_convert_fusion
  550.9 1.9 bitcast_multiply_fusion
  552.8 10.4 %scatter_custom_fusion = f32[128,512]{1,0:T(8,128)S(1)} fusion(s32[1536]{0:T(1024)S(1)} %fusion.21, f32[1536,512]{1,0:T(8,128)} %bitcast_multiply_fusion, f32[]{:T(128)} %constant.16.clone.1), kind=kCustom, calls=%fused_computation.27 | custom fusion | flops 786432 | bytes 262656 | tf_op jit(solution)/shard_map/scatter-add | solution.py:62
  563.3 0.7 convert_element_type.50
  (32 shorter events, 0.8 us)
Async XLA Ops:
  7.2 485.5 %copy-start = (bf16[2,1536,512]{2,1,0:T(8,128)(2,1)S(1)}, bf16[2,1536,512]{2,1,0:T(8,128)(2,1)}, u32[]{:S(2)}) copy-start(bf16[2,1536,512]{2,1,0:T(8,128)(2,1)} %param.15) | copy-start | bytes 9437188
  7.2 31.6 %all-gather.3.cloned.1.call-start = ((), (), s32[]{:S(2)}) async-start(), calls=%async_computation.3 | async-start | bytes 1179648 | tf_op jit(solution)/shard_map/all_gather | solution.py:36
  7.9 462.7 %all-gather.5.cloned.1.call-start = ((), (), s32[]{:S(2)}) async-start(), calls=%async_computation.4 | async-start | bytes 21233664 | tf_op jit(solution)/shard_map/all_gather | solution.py:55
  375.1 3.8 copy-start.3
  375.1 3.8 copy-start.4
  388.8 110.2 %all-to-all-start.2 = ((bf16[32,2,24]{2,1,0:T(2,128)(2,1)}), bf16[32,2,24]{2,1,0:T(2,128)(2,1)S(1)}, u32[]{:S(2)}, u32[]{:S(2)}) async-start(bf16[32,2,24]{2,1,0:T(2,128)(2,1)} %broadcast_select_fusion), calls=%async_computation.2 | async-start | bytes 32768 | tf_op jit(solution)/shard_map/all_to_all | solution.py:46
  497.7 11.7 %copy-start.1 = (s32[128,8]{0,1:T(8,128)S(1)}, s32[128,8]{0,1:T(8,128)}, u32[]{:S(2)}) copy-start(s32[128,8]{0,1:T(8,128)} %param.9) | copy-start | bytes 12292
  497.7 11.7 %copy-start.2 = (f32[128,8]{0,1:T(8,128)S(1)}, f32[128,8]{0,1:T(8,128)}, u32[]{:S(2)}) copy-start(f32[128,8]{0,1:T(8,128)} %param.10) | copy-start | bytes 12292
  499.1 50.0 %all-to-all-start.1 = ((bf16[2,32,24,512]{3,2,0,1:T(8,128)(2,1)}), bf16[2,32,24,512]{3,2,0,1:T(8,128)(2,1)}, u32[]{:S(2)}, u32[]{:S(2)}) async-start(bf16[2,32,24,512]{3,2,0,1:T(8,128)(2,1)} %copy.46), calls=%async_computation.1 | async-start | bytes 3145728 | tf_op jit(solution)/shard_map/all_to_all | solution.py:59
Sparse Core Ops, SparseCore 0:
  9.8 28.8 all-gather.2
  379.0 91.6 all-gather.4
where the time goes:
time: 572 us; the launch traced here: 571 us
  blocking collectives  286 us (50%)
  waiting for transfers between devices  127 us (22%)
  local copies, waits for them, and re-layouts  71.1 us (12%)
  matrix products  30.7 us (5%)
  other arithmetic  25.9 us (5%)
  starting transfers between devices  15.8 us (3%)
  between operations  14.3 us (2%)
    all_to_all x1, blocking collectives, on_device(): lax.all_to_all(rows.reshape(owners, local_exp, capacity, whole.shape[1]),...  286 us
    all_gather x1, waiting for transfers between devices, on_device(): piece = lax.all_gather(hidden, 'col', axis=3, tiled=True)  76.2 us
    all_gather x1, waiting for transfers between devices, on_device(): whole = lax.all_gather(tokens, 'col', axis=1, tiled=True)  26.8 us
    all_to_all x1, waiting for transfers between devices, on_device(): lax.all_to_all(expert_out, 'expert', split_axis=1, concat_axis=0, tiled=T...  23.4 us
    gather x1, local copies, waits for them, and re-layouts, on_device(): rows = jnp.take(whole, flat_token, axis=0)  23.4 us
    all_gather x1, local copies, waits for them, and re-layouts, on_device(): piece = lax.all_gather(hidden, 'col', axis=3, tiled=True)  22.1 us
  transfers between devices with their start and end apart: 4, of which 3 were waited for; matrix products, arithmetic and copies ran while one was open for 10% of the time, Pallas kernels for 0%

commit v1 on v0

--- a/solution.py
+++ b/solution.py
@@ -56,7 +56,12 @@
     block = jnp.einsum("escu,escv->euv", scaled, piece, preferred_element_type=jnp.float32)
     mixed_now = jnp.einsum("escv,evd->escd", piece, w_down, preferred_element_type=jnp.float32)
     expert_out = mixed_now.astype(jnp.bfloat16)
-    returned = lax.all_to_all(expert_out, "expert", split_axis=1, concat_axis=0, tiled=True)
+    returned = jnp.concatenate(
+        lax.all_to_all(
+            jnp.stack(jnp.split(expert_out, lax.axis_size("expert"), axis=1)), "expert", 0, 0
+        ),
+        axis=0,
+    )
     returned = returned.reshape(experts * capacity, d_local).astype(jnp.float32)
     combined = jnp.zeros((tok_rows, d_local), jnp.float32)
     combined = combined.at[flat_token].add(slot_coef.reshape(-1)[:, None] * returned)

time: 572 us -> 587 us (1.026)
  local copies, waits for them, and re-layouts: 71.1 us -> 90 us
    unnamed x10 -> x41, local copies, waits for them, and re-layouts: 0.03 us -> 19.7 us
  transfers between devices with their start and end apart: 4 -> 4, of which waited for: 3 -> 3; matrix products, arithmetic and copies ran while one was open for 10% -> 13% of each run, Pallas kernels for 0% -> 0%
where the time goes in v1:
time: 587 us; the launch traced here: 586 us
  blocking collectives  286 us (49%)
  waiting for transfers between devices  127 us (22%)
  local copies, waits for them, and re-layouts  90 us (15%)
  matrix products  30.7 us (5%)
  other arithmetic  22.7 us (4%)
  starting transfers between devices  16.2 us (3%)
  between operations  14.3 us (2%)
    all_to_all x1, blocking collectives, on_device(): lax.all_to_all(rows.reshape(owners, local_exp, capacity, whole.shape[1]),...  286 us
    all_gather x1, waiting for transfers between devices, on_device(): piece = lax.all_gather(hidden, 'col', axis=3, tiled=True)  75.7 us
    all_gather x1, waiting for transfers between devices, on_device(): whole = lax.all_gather(tokens, 'col', axis=1, tiled=True)  26.8 us
    all_to_all x1, waiting for transfers between devices, on_device(): lax.all_to_all(jnp.stack(jnp.split(expert_out, lax.axis_size('expert'), a...  23.4 us
    gather x1, local copies, waits for them, and re-layouts, on_device(): rows = jnp.take(whole, flat_token, axis=0)  23.4 us
    all_gather x1, local copies, waits for them, and re-layouts, on_device(): piece = lax.all_gather(hidden, 'col', axis=3, tiled=True)  22.1 us
    unnamed x41, local copies, waits for them, and re-layouts  19.7 us
  transfers between devices with their start and end apart: 4, of which 3 were waited for; matrix products, arithmetic and copies ran while one was open for 13% of the time, Pallas kernels for 0%

profile of v1, /device:TPU:4, one launch (start us, length us, event | category | flops | bytes accessed | tf_op | source)
XLA Modules:
  0.0 586.3 jit_solution(7306169723808622970)
XLA Ops:
  7.2 0.7 all-gather.3.cloned.1.call-update
  8.0 0.9 fusion.20
  9.3 1.2 select_reduce_fusion
  10.6 1.2 fusion.19
  11.9 26.8 %all-gather.3.cloned.1.call-done = bf16[128,4096]{1,0:T(8,128)(2,1)} async-done(((bf16[128,512]{1,0:T(8,128)(2,1)}), bf16[128,4096]{1,0:T(8,128)(2,1)}) %all-gather.3.cloned.1.call-update) | async-done | bytes 1048592 | tf_op jit(solution)/shard_map/all_gather | solution.py:36
  38.8 23.4 %gather_fusion = bf16[1536,4096]{1,0:T(8,128)(2,1)} fusion(bf16[128,4096]{1,0:T(8,128)(2,1)} %all-gather.3.cloned.1.call-done, s32[2048]{0:T(1024)S(1)} %pad_clamp_fusion.1), kind=kCustom, calls=%fused_computation | custom fusion | bytes 25171968 | tf_op jit(solution)/shard_map/jit(_take)/gather | solution.py:37
  62.2 6.7 %select_select_fusion = bf16[32,2,24,4096]{3,2,1,0:T(8,128)(2,1)S(1)} fusion(bf16[32,2,24,4096]{3,2,1,0:T(8,128)(2,1)} %bitcast.234, pred[32,2,24]{2,1,0:T(4,128)(4,1)S(1)} %compare_and_fusion, pred[32,2,24]{2,1,0:T(4,128)(4,1)S(1)} %broadcast_in_dim.95), kind=kLoop, calls=%fused_computation.4 | loop fusion | flops 12582912 | bytes 25168896 | tf_op jit(solution)/shard_map/jit(_where)/select_n | solution.py:38
  68.9 285.7 %all_to_all.15 = bf16[32,2,24,4096]{3,2,1,0:T(8,128)(2,1)} all-to-all(bf16[32,2,24,4096]{3,2,1,0:T(8,128)(2,1)S(1)} %select_select_fusion), channel_id=1, replica_groups=mesh['expert'=32,'col'=8] {'expert'}, dimensions={0} | all-to-all | bytes 25165824 | tf_op jit(solution)/shard_map/all_to_all | solution.py:39
  354.6 10.1 %fusion.2 = f32[2,32,24,192]{3,2,1,0:T(8,128)} fusion(bf16[32,2,24,4096]{3,2,1,0:T(8,128)(2,1)} %all_to_all.15, bf16[2,192,4096]{2,1,0:T(8,128)(2,1)} %param.13), kind=kOutput, calls=%fused_computation.7 | convolution fusion | flops 2415919104 | bytes 16908288 | tf_op jit(solution)/shard_map/seck,efk->escf/dot_general | solution.py:47
  364.7 10.5 %multiply_convert_fusion.1 = bf16[2,32,24,192]{3,2,1,0:T(8,128)(2,1)} fusion(f32[2,32,24,192]{3,2,1,0:T(8,128)} %fusion.2, bf16[2,192,4096]{2,1,0:T(8,128)(2,1)} %param.14, bf16[32,2,24,4096]{3,2,1,0:T(8,128)(2,1)} %all_to_all.15), kind=kOutput, calls=%fused_computation.18 | convolution fusion | flops 2417688576 | bytes 17498112 | tf_op jit(solution)/shard_map/seck,efk->escf/dot_general | solution.py:48
  375.1 3.7 copy.135
  379.6 9.0 %gather_fusion.1 = bf16[1536]{0:T(1024)(128)(2,1)S(1)} fusion(bf16[128]{0:T(256)(128)(2,1)S(1)} %select_reduce_fusion.2, s32[2048]{0:T(1024)S(1)} %pad_clamp_fusion), kind=kCustom, calls=%fused_computation.1 | custom fusion | bytes 12288 | tf_op jit(solution)/shard_map/gather | solution.py:28
  388.7 0.6 broadcast_select_fusion
  389.3 5.6 all-to-all-start.2
  394.9 75.7 %all-gather.5.cloned.1.call-done = bf16[2,32,24,1536]{1,2,0,3:T(8,128)(2,1)} async-done(((bf16[2,32,24,192]{1,2,0,3:T(8,128)(2,1)}), bf16[2,32,24,1536]{1,2,0,3:T(8,128)(2,1)}) %all-gather.5.cloned.1.call-update) | async-done | bytes 4718608 | tf_op jit(solution)/shard_map/all_gather | solution.py:55
  470.6 22.1 %copy.136 = bf16[2,32,24,1536]{3,2,1,0:T(8,128)(2,1)} copy(bf16[2,32,24,1536]{1,2,0,3:T(8,128)(2,1)} %all-gather.5.cloned.1.call-done) | data formatting | bytes 9437184 | tf_op jit(solution)/shard_map/all_gather | solution.py:55
  492.7 5.0 fusion.9
  497.7 0.6 constant_dynamic-update-slice_fusion.31
  500.2 0.6 constant_dynamic-update-slice_fusion.27
  502.0 0.6 constant_dynamic-update-slice_fusion.24
  502.6 0.6 constant_dynamic-update-slice_fusion.23
  508.2 0.6 constant_dynamic-update-slice_fusion.14
  510.1 0.6 constant_dynamic-update-slice_fusion.11
  513.2 0.6 constant_dynamic-update-slice_fusion.6
  515.6 0.6 constant_dynamic-update-slice_fusion.2
  516.2 0.6 constant_dynamic-update-slice_fusion.1
  517.5 10.5 %all-to-all-start.1 = ((bf16[32,2,1,24,512]{4,3,1,2,0:T(8,128)(2,1)}), bf16[32,2,1,24,512]{4,3,1,2,0:T(8,128)(2,1)}, u32[]{:S(2)}, u32[]{:S(2)}) async-start(bf16[32,2,1,24,512]{4,3,1,2,0:T(8,128)(2,1)} %constant_dynamic-update-slice_fusion), calls=%async_computation.1 | async-start | bytes 3145728 | tf_op jit(solution)/shard_map/all_to_all | solution.py:60
  528.5 10.7 %gather_fusion.2 = f32[1536]{0:T(1024)S(1)} fusion(f32[64,128]{0,1:T(8,128)S(1)} %bitcast.233, s32[1536]{0:T(1024)S(1)} %reshape.132), kind=kCustom, calls=%fused_computation.2 | custom fusion | bytes 24576 | tf_op jit(solution)/shard_map/jit(take_along_axis)/gather | solution.py:32
  539.2 5.2 convolution_bitcast_fusion
  544.4 23.4 %all-to-all-done.1 = bf16[32,2,1,24,512]{4,3,1,2,0:T(8,128)(2,1)} async-done(((bf16[32,2,1,24,512]{4,3,1,2,0:T(8,128)(2,1)}), bf16[32,2,1,24,512]{4,3,1,2,0:T(8,128)(2,1)}, u32[]{:S(2)}, u32[]{:S(2)}) %all-to-all-start.1) | async-done | bytes 1572896 | tf_op jit(solution)/shard_map/all_to_all | solution.py:60
  567.8 11.0 %scatter_custom_fusion = f32[128,512]{1,0:T(8,128)S(1)} fusion(s32[1536]{0:T(1024)S(1)} %fusion.22, bf16[1536,512]{1,0:T(8,128)(2,1)} %bitcast.51, f32[1536]{0:T(1024)S(1)} %select_select_fusion.1, f32[]{:T(128)} %constant.16.clone.1), kind=kCustom, calls=%fused_computation.10 | custom fusion | flops 2359296 | bytes 1843204 | tf_op jit(solution)/shard_map/scatter-add | solution.py:67
  578.8 0.7 convert_element_type.42
  (61 shorter events, 16.2 us)
Async XLA Ops:
  7.2 485.5 %copy-start = (bf16[2,1536,512]{2,1,0:T(8,128)(2,1)S(1)}, bf16[2,1536,512]{2,1,0:T(8,128)(2,1)}, u32[]{:S(2)}) copy-start(bf16[2,1536,512]{2,1,0:T(8,128)(2,1)} %param.15) | copy-start | bytes 9437188
  7.2 31.6 %all-gather.3.cloned.1.call-start = ((), (), s32[]{:S(2)}) async-start(), calls=%async_computation.3 | async-start | bytes 1179648 | tf_op jit(solution)/shard_map/all_gather | solution.py:36
  7.9 462.7 %all-gather.5.cloned.1.call-start = ((), (), s32[]{:S(2)}) async-start(), calls=%async_computation.4 | async-start | bytes 21233664 | tf_op jit(solution)/shard_map/all_gather | solution.py:55
  378.8 0.7 copy-start.3
  378.8 0.7 copy-start.4
  389.3 128.2 %all-to-all-start.2 = ((bf16[32,2,24]{2,1,0:T(2,128)(2,1)}), bf16[32,2,24]{2,1,0:T(2,128)(2,1)S(1)}, u32[]{:S(2)}, u32[]{:S(2)}) async-start(bf16[32,2,24]{2,1,0:T(2,128)(2,1)} %broadcast_select_fusion), calls=%async_computation.2 | async-start | bytes 32768 | tf_op jit(solution)/shard_map/all_to_all | solution.py:46
  517.5 10.7 %copy-start.1 = (s32[128,8]{0,1:T(8,128)S(1)}, s32[128,8]{0,1:T(8,128)}, u32[]{:S(2)}) copy-start(s32[128,8]{0,1:T(8,128)} %param.9) | copy-start | bytes 12292
  517.5 10.8 %copy-start.2 = (f32[128,8]{0,1:T(8,128)S(1)}, f32[128,8]{0,1:T(8,128)}, u32[]{:S(2)}) copy-start(f32[128,8]{0,1:T(8,128)} %param.10) | copy-start | bytes 12292
  517.5 50.3 %all-to-all-start.1 = ((bf16[32,2,1,24,512]{4,3,1,2,0:T(8,128)(2,1)}), bf16[32,2,1,24,512]{4,3,1,2,0:T(8,128)(2,1)}, u32[]{:S(2)}, u32[]{:S(2)}) async-start(bf16[32,2,1,24,512]{4,3,1,2,0:T(8,128)(2,1)} %constant_dynamic-update-slice_fusion), calls=%async_computation.1 | async-start | bytes 3145728 | tf_op jit(solution)/shard_map/all_to_all | solution.py:60
Sparse Core Ops, SparseCore 0:
  9.8 28.8 all-gather.2
  379.0 91.6 all-gather.4
